TPU v7x, 32 devices: a whole 2x2x4 slice. The times are simulated.
32 devices in a mesh: tx: 8 (over z, y), ty: 4 (over x, core).
Axes of the slice: x: 2, y: 2, z: 4, core: 2. Of those that a mesh axis runs over, the one named last changes fastest.
Arguments:
- concentration: float32 [64, 64, 256], P('tx', 'ty'), may hold values from -6 to 6
- source: float32 [64, 64, 256], P('tx', 'ty'), may hold values from -4 to 4
- material: int32 [64, 64, 256], P('tx', 'ty'), may hold values from 0 to 7
Outputs:
- updated: float32 [64, 64, 256], P('tx', 'ty')
All inputs are finite; a program needn't handle non-finite values.
Results may differ from a plain program's by a relative error of at most 0.00017.
Values sent between devices are 32-bit elements; how exact they have to be, the bound alone decides.
No kernel may reach another device: no remote copies, remote signals or barrier semaphores. Data moves between devices by JAX's collectives and lax.ppermute only.
A program may use at most 128 MiB of HBM per device.

v0:
```python
import jax
import jax.numpy as jnp
from jax import lax
from jax.sharding import PartitionSpec as P

mass_rate = 0.001
relax_weight = 0.8
diffusivities = (0.15, 0.3, 0.5, 0.8, 1.2, 2.0, 3.2, 5.0)


def with_halo(cells, sides, width):
    for axis, dim in sides:
        count = lax.axis_size(axis)
        head = lax.slice_in_dim(cells, 0, width, axis=dim)
        tail = lax.slice_in_dim(cells, cells.shape[dim] - width, cells.shape[dim], axis=dim)
        cells = jnp.concatenate(
            [
                lax.ppermute(tail, axis, [(i, (i + 1) % count) for i in range(count)]),
                cells,
                lax.ppermute(head, axis, [((i + 1) % count, i) for i in range(count)]),
            ],
            axis=dim,
        )
    return cells


def lookup(material):
    result = jnp.zeros(material.shape, jnp.float32)
    for slot_id, coeff_value in enumerate(diffusivities):
        result = jnp.where(material == slot_id, jnp.float32(coeff_value), result)
    return result


def couplings(kappa_pad, scales):
    scale_x, scale_y, scale_z = scales
    centre = kappa_pad[1:-1, 1:-1]
    return [
        0.5 * scale_x * (centre + kappa_pad[2:, 1:-1]),
        0.5 * scale_x * (centre + kappa_pad[:-2, 1:-1]),
        0.5 * scale_y * (centre + kappa_pad[1:-1, 2:]),
        0.5 * scale_y * (centre + kappa_pad[1:-1, :-2]),
        0.5 * scale_z * (centre + jnp.roll(centre, -1, axis=2)),
        0.5 * scale_z * (centre + jnp.roll(centre, 1, axis=2)),
    ]


def diagonal_of(coupled):
    summed = mass_rate + coupled[0]
    for coupled_term in coupled[1:]:
        summed = summed + coupled_term
    return summed


def operate(field_pad, coupled, diagonal):
    centre = field_pad[1:-1, 1:-1]
    beside_all = (
        field_pad[2:, 1:-1],
        field_pad[:-2, 1:-1],
        field_pad[1:-1, 2:],
        field_pad[1:-1, :-2],
        jnp.roll(centre, -1, axis=2),
        jnp.roll(centre, 1, axis=2),
    )
    off_sum = coupled[0] * beside_all[0]
    for number in range(1, 6):
        off_sum = off_sum + coupled[number] * beside_all[number]
    return diagonal * centre - off_sum


def sweep(field_pad, forcing, coupled, diagonal):
    centre = field_pad[1:-1, 1:-1]
    return centre + relax_weight * (forcing - operate(field_pad, coupled, diagonal)) / diagonal


def restrict(cells, ratios=(2, 2, 2)):
    size_x, size_y, size_z = cells.shape
    ratio_x, ratio_y, ratio_z = ratios
    grouped = cells.reshape(
        size_x // ratio_x, ratio_x, size_y // ratio_y, ratio_y, size_z // ratio_z, ratio_z
    )
    return jnp.sum(grouped, axis=(1, 3, 5)) * (1.0 / (ratio_x * ratio_y * ratio_z))


def prolong(coarse, ratios=(2, 2, 2)):
    return jnp.repeat(jnp.repeat(jnp.repeat(coarse, ratios[0], 0), ratios[1], 1), ratios[2], 2)


def wrap_pad(cells):
    return jnp.pad(cells, ((1, 1), (1, 1), (0, 0)), mode="wrap")


def scales_of(spacing):
    return tuple((1.0 / (step_size * step_size) for step_size in spacing))


def next_ratios(shape):
    return tuple((2 for extent in shape))


def exact_solve(forcing, coupled, diagonal):
    shape = forcing.shape
    cells = forcing.size
    basis = jnp.eye(cells, dtype=forcing.dtype).reshape((cells,) + shape)
    matrix = jax.vmap(lambda unit: operate(wrap_pad(unit), coupled, diagonal).reshape(cells))(basis)
    factor = jnp.linalg.cholesky(matrix)
    solved = jax.scipy.linalg.cho_solve((factor, True), forcing.reshape(cells))
    return solved.reshape(shape)


def coarse_solve(forcing, kappa, spacing):
    coupled = couplings(wrap_pad(kappa), scales_of(spacing))
    diagonal = diagonal_of(coupled)
    ratios = next_ratios(forcing.shape)
    if forcing.size <= 64 or ratios == (1, 1, 1):
        return exact_solve(forcing, coupled, diagonal)
    current = relax_weight * forcing / diagonal
    current = sweep(wrap_pad(current), forcing, coupled, diagonal)
    residual = forcing - operate(wrap_pad(current), coupled, diagonal)
    wider = tuple((step_size * ratio for step_size, ratio in zip(spacing, ratios)))
    correction = coarse_solve(restrict(residual, ratios), restrict(kappa, ratios), wider)
    current = current + prolong(correction, ratios)
    for repeat in range(2):
        current = sweep(wrap_pad(current), forcing, coupled, diagonal)
    return current


def grid_rim(cells, rim_width):
    return with_halo(cells, (("tx", 0), ("ty", 1)), rim_width)


def grid_ops(kappa_two, scales):
    wide = couplings(kappa_two, scales)
    wide_diag = diagonal_of(wide)
    inner = [coupled_term[1:-1, 1:-1] for coupled_term in wide]
    return (wide, wide_diag, inner, wide_diag[1:-1, 1:-1])


def smooth_twice(current, forcing, operators):
    wide, wide_diag, inner, inner_diag = operators
    for repeat in range(2):
        current = sweep(grid_rim(current, 1), forcing, inner, inner_diag)
    return current


def descend(forcing, operators):
    inner, inner_diag = (operators[2], operators[3])
    current = relax_weight * forcing / inner_diag
    current = sweep(grid_rim(current, 1), forcing, inner, inner_diag)
    residual = forcing - operate(grid_rim(current, 1), inner, inner_diag)
    return (current, residual)


def fetch_coarse(forcing_tile, kappa_tile):
    along_y = (
        lax.all_gather(forcing_tile, "ty", axis=1, tiled=True),
        lax.all_gather(kappa_tile, "ty", axis=1, tiled=True),
    )
    whole = (
        lax.all_gather(along_y[0], "tx", axis=0, tiled=True),
        lax.all_gather(along_y[1], "tx", axis=0, tiled=True),
    )
    return (whole[0], whole[1])


def shards(concentration, source, material):
    kappa_wide = with_halo(lookup(material), (("tx", 0), ("ty", 1)), 8)
    kappa_mid = restrict(kappa_wide)
    kappa_low = restrict(kappa_mid)
    kappa_base = restrict(kappa_low)
    top_ops = grid_ops(kappa_wide[6:-6, 6:-6], (1.0, 1.0, 1.0))
    mid_ops = grid_ops(kappa_mid[2:-2, 2:-2], (0.25, 0.25, 0.25))
    low_ops = grid_ops(kappa_low, (0.0625, 0.0625, 0.0625))
    forcing_top = mass_rate * concentration + source
    current_top = smooth_twice(concentration, forcing_top, top_ops)
    residual_top = forcing_top - operate(grid_rim(current_top, 1), top_ops[2], top_ops[3])
    forcing_mid = restrict(residual_top)
    current_mid, residual_mid = descend(forcing_mid, mid_ops)
    forcing_low = restrict(residual_mid)
    current_low, residual_low = descend(forcing_low, low_ops)
    forcing_base = restrict(residual_low)
    forcing_whole, kappa_whole = fetch_coarse(forcing_base, kappa_base[1:-1, 1:-1])
    solved_whole = coarse_solve(forcing_whole, kappa_whole, (8.0, 8.0, 8.0))
    part_x, part_y, part_z = forcing_base.shape
    start_x = lax.axis_index("tx") * part_x
    start_y = lax.axis_index("ty") * part_y
    current_base = lax.dynamic_slice(
        solved_whole, (start_x, start_y, jnp.int32(0)), (part_x, part_y, part_z)
    )
    current_low = current_low + prolong(current_base)
    current_low = smooth_twice(current_low, forcing_low, low_ops)
    current_mid = current_mid + prolong(current_low)
    current_mid = smooth_twice(current_mid, forcing_mid, mid_ops)
    current_top = current_top + prolong(current_mid)
    return smooth_twice(current_top, forcing_top, top_ops)


def solution(mesh):
    placed = (P("tx", "ty", None), P("tx", "ty", None), P("tx", "ty", None))
    return jax.shard_map(
        shards, mesh=mesh, in_specs=placed, out_specs=P("tx", "ty", None), check_vma=False
    )
```

profile of v0, /device:TPU:0, one launch (start us, length us, event | category | flops | bytes accessed | tf_op | source)
XLA Modules:
  0.0 330.1 jit_solution(3862219390328763433)
XLA Ops:
  1.0 3.0 collective-permute-start
  4.1 3.1 collective-permute-start.1
  7.9 4.7 %collective-permute-start.4 = (f32[1,16,256]{2,1,0:T(8,128)S(1)}, f32[1,16,256]{2,1,0:T(8,128)S(1)}, u32[]{:S(2)}, u32[]{:S(2)}) collective-permute-start(f32[1,16,256]{2,1,0:T(8,128)S(1)} %get-tuple-element.71), channel_id=1, source_target_pairs={{4,0},{8,4},{12,8},{16,12},{20,16},{24,20},{28,24},{0,28},{5,1},{9... | collective-permute-start | bytes 49160 | tf_op jit(solution)/shard_map/ppermute | solution.py:20
  12.6 1.1 fusion.384
  17.8 1.7 collective-permute-start.3
  20.1 3.0 collective-permute-done.2
  23.1 1.1 collective-permute-done.3
  25.8 51.6 %reshape.179 = f32[12,2,16,2,128,2]{5,4,3,2,1,0:T(8,128)} reshape(f32[24,32,256]{2,1,0:T(8,128)S(1)} %pad_maximum_fusion) | data formatting | bytes 1572864 | tf_op jit(solution)/shard_map/reshape | solution.py:78
  77.4 17.8 %reduce_sum.98 = f32[12,16,128]{2,1,0:T(8,128)S(1)} reduce(f32[12,2,16,2,128,2]{5,4,3,2,1,0:T(8,128)} %reshape.179, f32[]{:T(128)} %constant.121.clone.1), dimensions={1,3,5}, to_apply=%region_1.2 | reduce | flops 172032 | bytes 884740 | tf_op jit(solution)/shard_map/reduce_sum | solution.py:81
  96.1 7.6 %mul.837 = f32[6,2,8,2,64,2]{5,4,3,2,1,0:T(8,128)} reshape(f32[12,16,128]{2,1,0:T(8,128)S(1)} %broadcast_multiply_fusion) | data formatting | bytes 196608 | tf_op jit(solution)/shard_map/mul | solution.py:81
  103.7 3.3 reduce_sum.100
  109.3 5.3 %all_gather.14 = f32[1,8,32]{2,0,1:T(1,128)S(1)} all-gather(f32[1,2,32]{2,0,1:T(1,128)S(1)} %bitcast.82), channel_id=1, replica_groups=mesh['tx'=8,'ty'=4] {'ty'}, dimensions={1}, use_global_device_ids=true | all-gather | bytes 1280 | tf_op jit(solution)/shard_map/all_gather | solution.py:156
  114.7 30.6 %all_gather.15 = f32[8,8,32]{2,1,0:T(8,128)S(1)} all-gather(f32[1,8,32]{2,1,0:T(8,128)S(1)} %bitcast.76), channel_id=1, replica_groups=mesh['tx'=8,'ty'=4] {'tx'}, dimensions={0}, use_global_device_ids=true | all-gather | bytes 9216 | tf_op jit(solution)/shard_map/all_gather | solution.py:160
  148.8 1.5 collective-permute-start.8
  151.2 2.9 cholesky.16
  157.7 3.1 custom-call.10
  161.0 4.2 %collective-permute-start.12 = (f32[1,16,256]{2,1,0:T(8,128)S(1)}, f32[1,16,256]{2,1,0:T(8,128)S(1)}, u32[]{:S(2)}, u32[]{:S(2)}) collective-permute-start(f32[1,16,256]{2,1,0:T(8,128)S(1)} %get-tuple-element.60), channel_id=1, source_target_pairs={{4,0},{8,4},{12,8},{16,12},{20,16},{24,20},{28,24},{0,28},{5,1},{9... | collective-permute-start | bytes 49160 | tf_op jit(solution)/shard_map/ppermute | solution.py:20
  165.4 1.3 collective-permute-done.12
  166.7 5.0 %collective-permute-done.13 = f32[1,16,256]{2,1,0:T(8,128)S(1)} collective-permute-done((f32[1,16,256]{2,1,0:T(8,128)S(1)}, f32[1,16,256]{2,1,0:T(8,128)S(1)}, u32[]{:S(2)}, u32[]{:S(2)}) %collective-permute-start.13) | collective-permute-done | bytes 16416 | tf_op jit(solution)/shard_map/ppermute | solution.py:18
  173.2 1.8 collective-permute-done.15
  175.2 9.8 %reshape.178 = f32[4,2,8,2,128,2]{5,4,3,2,1,0:T(8,128)} reshape(f32[8,16,256]{2,1,0:T(8,128)S(1)} %fusion.41) | data formatting | bytes 262144 | tf_op jit(solution)/shard_map/reshape | solution.py:78
  185.0 4.0 %reduce_sum.97 = f32[4,8,128]{2,1,0:T(8,128)S(1)} reduce(f32[4,2,8,2,128,2]{5,4,3,2,1,0:T(8,128)} %reshape.178, f32[]{:T(128)} %constant.121.clone.1), dimensions={1,3,5}, to_apply=%region_0.1 | reduce | flops 28672 | bytes 147460 | tf_op jit(solution)/shard_map/reduce_sum | solution.py:81
  189.2 1.9 collective-permute-start.17
  191.2 1.5 collective-permute-done.16
  192.8 2.8 collective-permute-done.17
  196.9 1.8 collective-permute-done.19
  198.8 2.0 collective-permute-start.21
  200.9 1.5 collective-permute-done.20
  202.4 2.8 collective-permute-done.21
  206.5 1.8 collective-permute-done.23
  209.8 1.8 collective-permute-start.25
  211.7 1.5 collective-permute-done.24
  213.2 2.9 collective-permute-done.25
  217.5 1.8 collective-permute-done.27
  219.4 2.0 collective-permute-start.29
  221.5 1.5 collective-permute-done.28
  223.0 2.8 collective-permute-done.29
  227.1 1.8 collective-permute-done.31
  229.2 5.1 %all-gather.2 = f32[4,2,32]{2,1,0:T(2,128)S(1)} all-gather(f32[1,2,32]{2,1,0:T(2,128)S(1)} %multiply_bitcast_fusion), channel_id=2, replica_groups=mesh['tx'=8,'ty'=4] {'ty'}, dimensions={0}, use_global_device_ids=true | all-gather | bytes 1280 | tf_op jit(solution)/shard_map/all_gather | solution.py:155
  234.2 30.6 %all-gather.1 = f32[64,32]{1,0:T(8,128)S(1)} all-gather(f32[8,32]{1,0:T(8,128)S(1)} %bitcast.77), channel_id=3, replica_groups=mesh['tx'=8,'ty'=4] {'tx'}, dimensions={0}, use_global_device_ids=true | all-gather | bytes 9216 | tf_op jit(solution)/shard_map/all_gather | solution.py:159
  269.9 2.0 collective-permute-start.33
  271.9 1.5 collective-permute-done.32
  273.4 2.8 collective-permute-done.33
  277.6 1.8 collective-permute-done.35
  279.5 2.0 collective-permute-start.37
  281.6 1.5 collective-permute-done.36
  283.1 2.8 collective-permute-done.37
  287.2 1.8 collective-permute-done.39
  289.4 2.0 collective-permute-start.41
  291.5 1.5 collective-permute-done.40
  293.0 2.8 collective-permute-done.41
  297.1 1.8 collective-permute-done.43
  299.0 2.0 collective-permute-start.45
  301.1 1.5 collective-permute-done.44
  302.6 2.8 collective-permute-done.45
  306.7 1.8 collective-permute-done.47
  309.4 2.0 collective-permute-start.49
  311.5 1.6 collective-permute-done.48
  313.1 2.8 collective-permute-done.49
  317.4 1.8 collective-permute-done.51
  319.5 2.0 collective-permute-start.53
  321.6 1.6 collective-permute-done.52
  323.2 2.8 collective-permute-done.53
  327.4 1.8 collective-permute-done.55
  (301 shorter events, 45.4 us)
Async XLA Ops:
  1.0 16.6 %collective-permute-start = (f32[8,16,256]{2,1,0:T(8,128)S(1)}, f32[8,16,256]{2,1,0:T(8,128)S(1)}, u32[]{:S(2)}, u32[]{:S(2)}) collective-permute-start(f32[8,16,256]{2,1,0:T(8,128)S(1)} %select_select_fusion), channel_id=1, source_target_pairs={{0,4},{4,8},{8,12},{12,16},{16,20},{20,24},{24,28},{28,0},{1,5},{5... | collective-permute-start | bytes 393224 | tf_op jit(solution)/shard_map/ppermute | solution.py:18
  4.1 13.5 %collective-permute-start.1 = (f32[8,16,256]{2,1,0:T(8,128)S(1)}, f32[8,16,256]{2,1,0:T(8,128)S(1)}, u32[]{:S(2)}, u32[]{:S(2)}) collective-permute-start(f32[8,16,256]{2,1,0:T(8,128)S(1)} %select_select_fusion), channel_id=1, source_target_pairs={{4,0},{8,4},{12,8},{16,12},{20,16},{24,20},{28,24},{0,28},{5,1},{9... | collective-permute-start | bytes 393224 | tf_op jit(solution)/shard_map/ppermute | solution.py:20
  7.9 8.7 %collective-permute-start.5 = (f32[1,16,256]{2,1,0:T(8,128)S(1)}, f32[1,16,256]{2,1,0:T(8,128)S(1)}, u32[]{:S(2)}, u32[]{:S(2)}) collective-permute-start(f32[1,16,256]{2,1,0:T(8,128)S(1)} %get-tuple-element.72), channel_id=1, source_target_pairs={{0,4},{4,8},{8,12},{12,16},{16,20},{20,24},{24,28},{28,0},{1,5},{5... | collective-permute-start | bytes 49160 | tf_op jit(solution)/shard_map/ppermute | solution.py:18
  7.9 9.6 %collective-permute-start.4 = (f32[1,16,256]{2,1,0:T(8,128)S(1)}, f32[1,16,256]{2,1,0:T(8,128)S(1)}, u32[]{:S(2)}, u32[]{:S(2)}) collective-permute-start(f32[1,16,256]{2,1,0:T(8,128)S(1)} %get-tuple-element.71), channel_id=1, source_target_pairs={{4,0},{8,4},{12,8},{16,12},{20,16},{24,20},{28,24},{0,28},{5,1},{9... | collective-permute-start | bytes 49160 | tf_op jit(solution)/shard_map/ppermute | solution.py:20
  17.7 5.4 %collective-permute-start.2 = (f32[24,8,256]{2,1,0:T(8,128)S(1)}, f32[24,8,256]{2,1,0:T(8,128)S(1)}, u32[]{:S(2)}, u32[]{:S(2)}) collective-permute-start(f32[24,8,256]{2,1,0:T(8,128)S(1)} %get-tuple-element.31), channel_id=1, source_target_pairs={{0,1},{1,2},{2,3},{3,0},{4,5},{5,6},{6,7},{7,4},{8,9},{9,10},{10,1... | collective-permute-start | bytes 589832 | tf_op jit(solution)/shard_map/ppermute | solution.py:18
  17.8 6.4 %collective-permute-start.3 = (f32[24,8,256]{2,1,0:T(8,128)S(1)}, f32[24,8,256]{2,1,0:T(8,128)S(1)}, u32[]{:S(2)}, u32[]{:S(2)}) collective-permute-start(f32[24,8,256]{2,1,0:T(8,128)S(1)} %get-tuple-element.32), channel_id=1, source_target_pairs={{1,0},{2,1},{3,2},{0,3},{5,4},{6,5},{7,6},{4,7},{9,8},{10,9},{11,1... | collective-permute-start | bytes 589832 | tf_op jit(solution)/shard_map/ppermute | solution.py:20
  19.5 5.2 %collective-permute-start.6 = (f32[10,1,256]{2,1,0:T(1,128)S(1)}, f32[10,1,256]{2,1,0:T(1,128)S(1)}, u32[]{:S(2)}, u32[]{:S(2)}) collective-permute-start(f32[10,1,256]{2,1,0:T(1,128)S(1)} %get-tuple-element.41), channel_id=1, source_target_pairs={{1,0},{2,1},{3,2},{0,3},{5,4},{6,5},{7,6},{4,7},{9,8},{10,9},{11,1... | collective-permute-start | bytes 30728 | tf_op jit(solution)/shard_map/ppermute | solution.py:20
  19.6 5.2 %collective-permute-start.7 = (f32[10,1,256]{2,1,0:T(1,128)S(1)}, f32[10,1,256]{2,1,0:T(1,128)S(1)}, u32[]{:S(2)}, u32[]{:S(2)}) collective-permute-start(f32[10,1,256]{2,1,0:T(1,128)S(1)} %get-tuple-element.42), channel_id=1, source_target_pairs={{0,1},{1,2},{2,3},{3,0},{4,5},{5,6},{6,7},{7,4},{8,9},{9,10},{10,1... | collective-permute-start | bytes 30728 | tf_op jit(solution)/shard_map/ppermute | solution.py:18
  95.2 55.7 %copy-start.7 = (f32[32,1,2,8]{0,3,2,1:T(8,128)S(1)}, f32[32,1,2,8]{0,3,2,1:T(8,128)}, u32[]{:S(2)}) copy-start(f32[32,1,2,8]{0,3,2,1:T(8,128)} %copy-done.6) | copy-start | bytes 6148
  95.2 55.7 %copy-start.9 = (f32[32,1,2,8]{0,3,2,1:T(8,128)S(1)}, f32[32,1,2,8]{0,3,2,1:T(8,128)}, u32[]{:S(2)}) copy-start(f32[32,1,2,8]{0,3,2,1:T(8,128)} %copy-done.8) | copy-start | bytes 6148
  148.8 8.3 %collective-permute-start.8 = (f32[1,16,256]{2,1,0:T(8,128)}, f32[1,16,256]{2,1,0:T(8,128)S(1)}, u32[]{:S(2)}, u32[]{:S(2)}) collective-permute-start(f32[1,16,256]{2,1,0:T(8,128)} %get-tuple-element.66), channel_id=1, source_target_pairs={{4,0},{8,4},{12,8},{16,12},{20,16},{24,20},{28,24},{0,28},{5,1},{9... | collective-permute-start | bytes 49160 | tf_op jit(solution)/shard_map/ppermute | solution.py:20
  150.3 6.8 %collective-permute-start.9 = (f32[1,16,256]{2,1,0:T(8,128)}, f32[1,16,256]{2,1,0:T(8,128)S(1)}, u32[]{:S(2)}, u32[]{:S(2)}) collective-permute-start(f32[1,16,256]{2,1,0:T(8,128)} %get-tuple-element.65), channel_id=1, source_target_pairs={{0,4},{4,8},{8,12},{12,16},{16,20},{20,24},{24,28},{28,0},{1,5},{5... | collective-permute-start | bytes 49160 | tf_op jit(solution)/shard_map/ppermute | solution.py:18
  157.1 3.6 %collective-permute-start.10 = (f32[10,1,256]{2,1,0:T(1,128)S(1)}, f32[10,1,256]{2,1,0:T(1,128)S(1)}, u32[]{:S(2)}, u32[]{:S(2)}) collective-permute-start(f32[10,1,256]{2,1,0:T(1,128)S(1)} %get-tuple-element.39), channel_id=1, source_target_pairs={{1,0},{2,1},{3,2},{0,3},{5,4},{6,5},{7,6},{4,7},{9,8},{10,9},{11,1... | collective-permute-start | bytes 30728 | tf_op jit(solution)/shard_map/ppermute | solution.py:20
  157.2 3.6 %collective-permute-start.11 = (f32[10,1,256]{2,1,0:T(1,128)S(1)}, f32[10,1,256]{2,1,0:T(1,128)S(1)}, u32[]{:S(2)}, u32[]{:S(2)}) collective-permute-start(f32[10,1,256]{2,1,0:T(1,128)S(1)} %get-tuple-element.40), channel_id=1, source_target_pairs={{0,1},{1,2},{2,3},{3,0},{4,5},{5,6},{6,7},{7,4},{8,9},{9,10},{10,1... | collective-permute-start | bytes 30728 | tf_op jit(solution)/shard_map/ppermute | solution.py:18
  161.0 5.7 %collective-permute-start.12 = (f32[1,16,256]{2,1,0:T(8,128)S(1)}, f32[1,16,256]{2,1,0:T(8,128)S(1)}, u32[]{:S(2)}, u32[]{:S(2)}) collective-permute-start(f32[1,16,256]{2,1,0:T(8,128)S(1)} %get-tuple-element.60), channel_id=1, source_target_pairs={{4,0},{8,4},{12,8},{16,12},{20,16},{24,20},{28,24},{0,28},{5,1},{9... | collective-permute-start | bytes 49160 | tf_op jit(solution)/shard_map/ppermute | solution.py:20
  165.3 6.4 %collective-permute-start.13 = (f32[1,16,256]{2,1,0:T(8,128)S(1)}, f32[1,16,256]{2,1,0:T(8,128)S(1)}, u32[]{:S(2)}, u32[]{:S(2)}) collective-permute-start(f32[1,16,256]{2,1,0:T(8,128)S(1)} %get-tuple-element.59), channel_id=1, source_target_pairs={{0,4},{4,8},{8,12},{12,16},{16,20},{20,24},{24,28},{28,0},{1,5},{5... | collective-permute-start | bytes 49160 | tf_op jit(solution)/shard_map/ppermute | solution.py:18
  171.7 1.4 collective-permute-start.14
  171.8 3.1 collective-permute-start.15
  175.2 89.7 %copy-start.1 = (f32[8,8,1]{2,1,0:T(8,128)S(1)}, f32[8,8,1]{2,1,0:T(8,128)}, u32[]{:S(2)}) copy-start(f32[8,8,1]{2,1,0:T(8,128)} %get-tuple-element.109) | copy-start | bytes 772
  175.2 89.6 %copy-start.2 = (f32[8,8,1]{2,1,0:T(8,128)S(1)}, f32[8,8,1]{2,1,0:T(8,128)}, u32[]{:S(2)}) copy-start(f32[8,8,1]{2,1,0:T(8,128)} %get-tuple-element.110) | copy-start | bytes 772
  175.2 89.6 %copy-start.3 = (f32[8,8,31]{2,1,0:T(8,128)S(1)}, f32[8,8,31]{2,1,0:T(8,128)}, u32[]{:S(2)}) copy-start(f32[8,8,31]{2,1,0:T(8,128)} %get-tuple-element.111) | copy-start | bytes 23812
  175.2 89.6 %copy-start.4 = (f32[8,8,31]{2,1,0:T(8,128)S(1)}, f32[8,8,31]{2,1,0:T(8,128)}, u32[]{:S(2)}) copy-start(f32[8,8,31]{2,1,0:T(8,128)} %get-tuple-element.112) | copy-start | bytes 23812
  185.0 80.9 %copy-start.15 = (f32[4,4,1]{2,1,0:T(4,128)S(1)}, f32[4,4,1]{2,1,0:T(4,128)}, u32[]{:S(2)}) copy-start(f32[4,4,1]{2,1,0:T(4,128)} %get-tuple-element.191) | copy-start | bytes 196
  185.0 82.5 %copy-start.10 = (f32[1,32,32]{1,2,0:T(8,128)S(1)}, f32[1,32,32]{1,2,0:T(8,128)}, u32[]{:S(2)}) copy-start(f32[1,32,32]{1,2,0:T(8,128)} %custom-call.10) | copy-start | bytes 12292
  189.1 3.7 %collective-permute-start.16 = (f32[1,8,128]{2,1,0:T(8,128)S(1)}, f32[1,8,128]{2,1,0:T(8,128)S(1)}, u32[]{:S(2)}, u32[]{:S(2)}) collective-permute-start(f32[1,8,128]{2,1,0:T(8,128)S(1)} %get-tuple-element.162), channel_id=1, source_target_pairs={{4,0},{8,4},{12,8},{16,12},{20,16},{24,20},{28,24},{0,28},{5,1},{9... | collective-permute-start | bytes 12296 | tf_op jit(solution)/shard_map/ppermute | solution.py:20
  189.2 6.3 %collective-permute-start.17 = (f32[1,8,128]{2,1,0:T(8,128)S(1)}, f32[1,8,128]{2,1,0:T(8,128)S(1)}, u32[]{:S(2)}, u32[]{:S(2)}) collective-permute-start(f32[1,8,128]{2,1,0:T(8,128)S(1)} %get-tuple-element.161), channel_id=1, source_target_pairs={{0,4},{4,8},{8,12},{12,16},{16,20},{20,24},{24,28},{28,0},{1,5},{5... | collective-permute-start | bytes 12296 | tf_op jit(solution)/shard_map/ppermute | solution.py:18
  195.6 1.3 collective-permute-start.18
  195.6 3.1 collective-permute-start.19
  198.7 3.7 %collective-permute-start.20 = (f32[1,8,128]{2,1,0:T(8,128)S(1)}, f32[1,8,128]{2,1,0:T(8,128)S(1)}, u32[]{:S(2)}, u32[]{:S(2)}) collective-permute-start(f32[1,8,128]{2,1,0:T(8,128)S(1)} %get-tuple-element.156), channel_id=1, source_target_pairs={{4,0},{8,4},{12,8},{16,12},{20,16},{24,20},{28,24},{0,28},{5,1},{9... | collective-permute-start | bytes 12296 | tf_op jit(solution)/shard_map/ppermute | solution.py:20
  198.8 6.3 %collective-permute-start.21 = (f32[1,8,128]{2,1,0:T(8,128)S(1)}, f32[1,8,128]{2,1,0:T(8,128)S(1)}, u32[]{:S(2)}, u32[]{:S(2)}) collective-permute-start(f32[1,8,128]{2,1,0:T(8,128)S(1)} %get-tuple-element.155), channel_id=1, source_target_pairs={{0,4},{4,8},{8,12},{12,16},{16,20},{20,24},{24,28},{28,0},{1,5},{5... | collective-permute-start | bytes 12296 | tf_op jit(solution)/shard_map/ppermute | solution.py:18
  205.2 1.3 collective-permute-start.22
  205.2 3.1 collective-permute-start.23
  209.5 3.6 %collective-permute-start.24 = (f32[1,4,64]{2,1,0:T(4,128)S(1)}, f32[1,4,64]{2,1,0:T(4,128)S(1)}, u32[]{:S(2)}, u32[]{:S(2)}) collective-permute-start(f32[1,4,64]{2,1,0:T(4,128)S(1)} %get-tuple-element.226), channel_id=1, source_target_pairs={{4,0},{8,4},{12,8},{16,12},{20,16},{24,20},{28,24},{0,28},{5,1},{9... | collective-permute-start | bytes 3080 | tf_op jit(solution)/shard_map/ppermute | solution.py:20
  209.8 6.3 %collective-permute-start.25 = (f32[1,4,64]{2,1,0:T(4,128)S(1)}, f32[1,4,64]{2,1,0:T(4,128)S(1)}, u32[]{:S(2)}, u32[]{:S(2)}) collective-permute-start(f32[1,4,64]{2,1,0:T(4,128)S(1)} %get-tuple-element.225), channel_id=1, source_target_pairs={{0,4},{4,8},{8,12},{12,16},{16,20},{20,24},{24,28},{28,0},{1,5},{5... | collective-permute-start | bytes 3080 | tf_op jit(solution)/shard_map/ppermute | solution.py:18
  216.1 1.4 collective-permute-start.26
  216.2 3.1 collective-permute-start.27
  219.3 3.6 %collective-permute-start.28 = (f32[1,4,64]{2,1,0:T(4,128)S(1)}, f32[1,4,64]{2,1,0:T(4,128)S(1)}, u32[]{:S(2)}, u32[]{:S(2)}) collective-permute-start(f32[1,4,64]{2,1,0:T(4,128)S(1)} %get-tuple-element.216), channel_id=1, source_target_pairs={{4,0},{8,4},{12,8},{16,12},{20,16},{24,20},{28,24},{0,28},{5,1},{9... | collective-permute-start | bytes 3080 | tf_op jit(solution)/shard_map/ppermute | solution.py:20
  219.4 6.3 %collective-permute-start.29 = (f32[1,4,64]{2,1,0:T(4,128)S(1)}, f32[1,4,64]{2,1,0:T(4,128)S(1)}, u32[]{:S(2)}, u32[]{:S(2)}) collective-permute-start(f32[1,4,64]{2,1,0:T(4,128)S(1)} %get-tuple-element.215), channel_id=1, source_target_pairs={{0,4},{4,8},{8,12},{12,16},{16,20},{20,24},{24,28},{28,0},{1,5},{5... | collective-permute-start | bytes 3080 | tf_op jit(solution)/shard_map/ppermute | solution.py:18
  225.8 1.4 collective-permute-start.30
  225.8 3.1 collective-permute-start.31
  269.8 3.6 %collective-permute-start.32 = (f32[1,4,64]{2,1,0:T(4,128)S(1)}, f32[1,4,64]{2,1,0:T(4,128)S(1)}, u32[]{:S(2)}, u32[]{:S(2)}) collective-permute-start(f32[1,4,64]{2,1,0:T(4,128)S(1)} %get-tuple-element.212), channel_id=1, source_target_pairs={{4,0},{8,4},{12,8},{16,12},{20,16},{24,20},{28,24},{0,28},{5,1},{9... | collective-permute-start | bytes 3080 | tf_op jit(solution)/shard_map/ppermute | solution.py:20
  269.9 6.3 %collective-permute-start.33 = (f32[1,4,64]{2,1,0:T(4,128)S(1)}, f32[1,4,64]{2,1,0:T(4,128)S(1)}, u32[]{:S(2)}, u32[]{:S(2)}) collective-permute-start(f32[1,4,64]{2,1,0:T(4,128)S(1)} %get-tuple-element.211), channel_id=1, source_target_pairs={{0,4},{4,8},{8,12},{12,16},{16,20},{20,24},{24,28},{28,0},{1,5},{5... | collective-permute-start | bytes 3080 | tf_op jit(solution)/shard_map/ppermute | solution.py:18
  276.2 1.4 collective-permute-start.34
  276.3 3.1 collective-permute-start.35
  279.4 3.6 %collective-permute-start.36 = (f32[1,4,64]{2,1,0:T(4,128)S(1)}, f32[1,4,64]{2,1,0:T(4,128)S(1)}, u32[]{:S(2)}, u32[]{:S(2)}) collective-permute-start(f32[1,4,64]{2,1,0:T(4,128)S(1)} %get-tuple-element.206), channel_id=1, source_target_pairs={{4,0},{8,4},{12,8},{16,12},{20,16},{24,20},{28,24},{0,28},{5,1},{9... | collective-permute-start | bytes 3080 | tf_op jit(solution)/shard_map/ppermute | solution.py:20
  279.5 6.3 %collective-permute-start.37 = (f32[1,4,64]{2,1,0:T(4,128)S(1)}, f32[1,4,64]{2,1,0:T(4,128)S(1)}, u32[]{:S(2)}, u32[]{:S(2)}) collective-permute-start(f32[1,4,64]{2,1,0:T(4,128)S(1)} %get-tuple-element.205), channel_id=1, source_target_pairs={{0,4},{4,8},{8,12},{12,16},{16,20},{20,24},{24,28},{28,0},{1,5},{5... | collective-permute-start | bytes 3080 | tf_op jit(solution)/shard_map/ppermute | solution.py:18
  285.8 1.4 collective-permute-start.38
  285.9 3.1 collective-permute-start.39
  289.4 3.7 %collective-permute-start.40 = (f32[1,8,128]{2,1,0:T(8,128)S(1)}, f32[1,8,128]{2,1,0:T(8,128)S(1)}, u32[]{:S(2)}, u32[]{:S(2)}) collective-permute-start(f32[1,8,128]{2,1,0:T(8,128)S(1)} %get-tuple-element.144), channel_id=1, source_target_pairs={{4,0},{8,4},{12,8},{16,12},{20,16},{24,20},{28,24},{0,28},{5,1},{9... | collective-permute-start | bytes 12296 | tf_op jit(solution)/shard_map/ppermute | solution.py:20
  289.4 6.4 %collective-permute-start.41 = (f32[1,8,128]{2,1,0:T(8,128)S(1)}, f32[1,8,128]{2,1,0:T(8,128)S(1)}, u32[]{:S(2)}, u32[]{:S(2)}) collective-permute-start(f32[1,8,128]{2,1,0:T(8,128)S(1)} %get-tuple-element.143), channel_id=1, source_target_pairs={{0,4},{4,8},{8,12},{12,16},{16,20},{20,24},{24,28},{28,0},{1,5},{5... | collective-permute-start | bytes 12296 | tf_op jit(solution)/shard_map/ppermute | solution.py:18
  295.8 1.3 collective-permute-start.42
  295.8 3.1 collective-permute-start.43
  299.0 3.7 %collective-permute-start.44 = (f32[1,8,128]{2,1,0:T(8,128)S(1)}, f32[1,8,128]{2,1,0:T(8,128)S(1)}, u32[]{:S(2)}, u32[]{:S(2)}) collective-permute-start(f32[1,8,128]{2,1,0:T(8,128)S(1)} %get-tuple-element.138), channel_id=1, source_target_pairs={{4,0},{8,4},{12,8},{16,12},{20,16},{24,20},{28,24},{0,28},{5,1},{9... | collective-permute-start | bytes 12296 | tf_op jit(solution)/shard_map/ppermute | solution.py:20
  299.0 6.4 %collective-permute-start.45 = (f32[1,8,128]{2,1,0:T(8,128)S(1)}, f32[1,8,128]{2,1,0:T(8,128)S(1)}, u32[]{:S(2)}, u32[]{:S(2)}) collective-permute-start(f32[1,8,128]{2,1,0:T(8,128)S(1)} %get-tuple-element.137), channel_id=1, source_target_pairs={{0,4},{4,8},{8,12},{12,16},{16,20},{20,24},{24,28},{28,0},{1,5},{5... | collective-permute-start | bytes 12296 | tf_op jit(solution)/shard_map/ppermute | solution.py:18
  305.4 1.3 collective-permute-start.46
  305.4 3.1 collective-permute-start.47
  309.4 3.8 %collective-permute-start.48 = (f32[1,16,256]{2,1,0:T(8,128)S(1)}, f32[1,16,256]{2,1,0:T(8,128)S(1)}, u32[]{:S(2)}, u32[]{:S(2)}) collective-permute-start(f32[1,16,256]{2,1,0:T(8,128)S(1)} %get-tuple-element.54), channel_id=1, source_target_pairs={{4,0},{8,4},{12,8},{16,12},{20,16},{24,20},{28,24},{0,28},{5,1},{9... | collective-permute-start | bytes 49160 | tf_op jit(solution)/shard_map/ppermute | solution.py:20
  309.4 6.5 %collective-permute-start.49 = (f32[1,16,256]{2,1,0:T(8,128)S(1)}, f32[1,16,256]{2,1,0:T(8,128)S(1)}, u32[]{:S(2)}, u32[]{:S(2)}) collective-permute-start(f32[1,16,256]{2,1,0:T(8,128)S(1)} %get-tuple-element.53), channel_id=1, source_target_pairs={{0,4},{4,8},{8,12},{12,16},{16,20},{20,24},{24,28},{28,0},{1,5},{5... | collective-permute-start | bytes 49160 | tf_op jit(solution)/shard_map/ppermute | solution.py:18
  315.9 1.4 collective-permute-start.50
  316.0 3.1 collective-permute-start.51
  319.4 3.8 %collective-permute-start.52 = (f32[1,16,256]{2,1,0:T(8,128)S(1)}, f32[1,16,256]{2,1,0:T(8,128)S(1)}, u32[]{:S(2)}, u32[]{:S(2)}) collective-permute-start(f32[1,16,256]{2,1,0:T(8,128)S(1)} %get-tuple-element.48), channel_id=1, source_target_pairs={{4,0},{8,4},{12,8},{16,12},{20,16},{24,20},{28,24},{0,28},{5,1},{9... | collective-permute-start | bytes 49160 | tf_op jit(solution)/shard_map/ppermute | solution.py:20
  319.5 6.5 %collective-permute-start.53 = (f32[1,16,256]{2,1,0:T(8,128)S(1)}, f32[1,16,256]{2,1,0:T(8,128)S(1)}, u32[]{:S(2)}, u32[]{:S(2)}) collective-permute-start(f32[1,16,256]{2,1,0:T(8,128)S(1)} %get-tuple-element.47), channel_id=1, source_target_pairs={{0,4},{4,8},{8,12},{12,16},{16,20},{20,24},{24,28},{28,0},{1,5},{5... | collective-permute-start | bytes 49160 | tf_op jit(solution)/shard_map/ppermute | solution.py:18
  326.0 1.4 collective-permute-start.54
  326.0 3.1 collective-permute-start.55
  (12 other events, 445.7 us)
where the time goes:
time: 331 us; the launch traced here: 330 us
  local copies, waits for them, and re-layouts  88 us (27%)
  waiting for transfers between devices  81.2 us (25%)
  blocking collectives  71.6 us (22%)
  starting transfers between devices  46.7 us (14%)
  other arithmetic  41.1 us (12%)
    reshape x6, local copies, waits for them, and re-layouts, restrict(): cells.reshape(size_x // ratio_x, ratio_x, size_y // ratio_y, ratio_y, siz...  63 us
    ppermute x28, waiting for transfers between devices, with_halo(): lax.ppermute(tail, axis, [(i, (i + 1) % count) for i in range(count)])  55.2 us
    all_gather x1, blocking collectives, fetch_coarse(): lax.all_gather(along_y[1], 'tx', axis=0, tiled=True)  30.6 us
    all_gather x1, blocking collectives, fetch_coarse(): lax.all_gather(along_y[0], 'tx', axis=0, tiled=True)  30.6 us
    ppermute x28, starting transfers between devices, with_halo(): lax.ppermute(tail, axis, [(i, (i + 1) % count) for i in range(count)])  29.9 us
    reduce_sum x11, other arithmetic, restrict(): jnp.sum(grouped, axis=(1, 3, 5)) * (1.0 / (ratio_x * ratio_y * ratio_z))  26 us
    ppermute x28, waiting for transfers between devices, with_halo(): lax.ppermute(head, axis, [((i + 1) % count, i) for i in range(count)])  25.9 us
    ppermute x28, starting transfers between devices, with_halo(): lax.ppermute(head, axis, [((i + 1) % count, i) for i in range(count)])  16.8 us
  transfers between devices with their start and end apart: 56, of which 46 were waited for; matrix products, arithmetic and copies ran while one was open for 5% of the time, Pallas kernels for 0%

commit v1 on v0

--- a/solution.py
+++ b/solution.py
@@ -6,6 +6,27 @@
 mass_rate = 0.001
 relax_weight = 0.8
 diffusivities = (0.15, 0.3, 0.5, 0.8, 1.2, 2.0, 3.2, 5.0)
+
+
+def gather_around(x, axis, dim):
+    size, place, width = (lax.axis_size(axis), lax.axis_index(axis), x.shape[dim])
+    right = [(i, (i + 1) % size) for i in range(size)]
+    left = [(i, (i - 1) % size) for i in range(size)]
+    out = jnp.zeros((*x.shape[:dim], size * width, *x.shape[dim + 1 :]), x.dtype)
+    out = lax.dynamic_update_slice_in_dim(out, x, place * width, axis=dim)
+    from_left = from_right = x
+    halfway = size // 2
+    for step in range(1, halfway + 1):
+        from_left = lax.ppermute(from_left, axis, right)
+        out = lax.dynamic_update_slice_in_dim(
+            out, from_left, (place - step) % size * width, axis=dim
+        )
+        if step < size - halfway:
+            from_right = lax.ppermute(from_right, axis, left)
+            out = lax.dynamic_update_slice_in_dim(
+                out, from_right, (place + step) % size * width, axis=dim
+            )
+    return out
 
 
 def with_halo(cells, sides, width):
@@ -156,7 +177,7 @@
         lax.all_gather(kappa_tile, "ty", axis=1, tiled=True),
     )
     whole = (
-        lax.all_gather(along_y[0], "tx", axis=0, tiled=True),
+        gather_around(along_y[0], "tx", 0),
         lax.all_gather(along_y[1], "tx", axis=0, tiled=True),
     )
     return (whole[0], whole[1])

time: 331 us -> 343 us (1.036)
  blocking collectives: 71.6 us -> 41 us
  starting transfers between devices: 46.7 us -> 63.9 us
  other arithmetic: 41.1 us -> 50.4 us
  local copies, waits for them, and re-layouts: 88 us -> 97.2 us
  waiting for transfers between devices: 81.2 us -> 87.8 us
    all_gather x1 -> x0, blocking collectives: 30.6 us -> none  [fetch_coarse(): lax.all_gather(along_y[0], 'tx', axis=0, tiled=True)]
    ppermute x0 -> x7, starting transfers between devices: none -> 14.4 us  [the longest x3 14.4 us: gather_around(): from_right = lax.ppermute(from_right, axis, left)]
    ppermute x28, starting transfers between devices: 16.8 us -> 21.8 us  [with_halo(): lax.ppermute(head, axis, [((i + 1) % count, i) for i in range(count)])]
    add x15 -> x16, other arithmetic: 2.63 us -> 7.16 us  [sweep(): centre + relax_weight * (forcing - operate(field_pad, coupled, diagonal))...]
    slice x14 -> x21, local copies, waits for them, and re-layouts: 0.65 us -> 4.89 us  [wrap_pad(): return jnp.pad(cells, ((1, 1), (1, 1), (0, 0)), mode='wrap')]
    ppermute x28, waiting for transfers between devices: 55.2 us -> 59.2 us  [with_halo(): lax.ppermute(tail, axis, [(i, (i + 1) % count) for i in range(count)])]
  transfers between devices with their start and end apart: 56 -> 63, of which waited for: 46 -> 52; matrix products, arithmetic and copies ran while one was open for 5% -> 8% of each run, Pallas kernels for 0% -> 0%
where the time goes in v1:
time: 343 us; the launch traced here: 342 us
  local copies, waits for them, and re-layouts  97.2 us (28%)
  waiting for transfers between devices  87.8 us (26%)
  starting transfers between devices  63.9 us (19%)
  other arithmetic  50.4 us (15%)
  blocking collectives  41 us (12%)
    reshape x6, local copies, waits for them, and re-layouts, restrict(): cells.reshape(size_x // ratio_x, ratio_x, size_y // ratio_y, ratio_y, siz...  63 us
    ppermute x28, waiting for transfers between devices, with_halo(): lax.ppermute(tail, axis, [(i, (i + 1) % count) for i in range(count)])  59.2 us
    all_gather x1, blocking collectives, fetch_coarse(): lax.all_gather(along_y[1], 'tx', axis=0, tiled=True)  30.6 us
    ppermute x28, starting transfers between devices, with_halo(): lax.ppermute(tail, axis, [(i, (i + 1) % count) for i in range(count)])  27.7 us
    reduce_sum x11, other arithmetic, restrict(): jnp.sum(grouped, axis=(1, 3, 5)) * (1.0 / (ratio_x * ratio_y * ratio_z))  26.7 us
    ppermute x28, waiting for transfers between devices, with_halo(): lax.ppermute(head, axis, [((i + 1) % count, i) for i in range(count)])  25.9 us
    ppermute x28, starting transfers between devices, with_halo(): lax.ppermute(head, axis, [((i + 1) % count, i) for i in range(count)])  21.8 us
    ppermute x3, starting transfers between devices, gather_around(): from_right = lax.ppermute(from_right, axis, left)  14.4 us
  transfers between devices with their start and end apart: 63, of which 52 were waited for; matrix products, arithmetic and copies ran while one was open for 8% of the time, Pallas kernels for 0%

profile of v1, /device:TPU:0, one launch (start us, length us, event | category | flops | bytes accessed | tf_op | source)
XLA Modules:
  0.0 342.1 jit_solution(822182566495040133)
XLA Ops:
  1.0 3.0 collective-permute-start
  4.1 3.1 collective-permute-start.1
  7.9 4.7 %collective-permute-start.4 = (f32[1,16,256]{2,1,0:T(8,128)S(1)}, f32[1,16,256]{2,1,0:T(8,128)S(1)}, u32[]{:S(2)}, u32[]{:S(2)}) collective-permute-start(f32[1,16,256]{2,1,0:T(8,128)S(1)} %get-tuple-element.107), channel_id=1, source_target_pairs={{4,0},{8,4},{12,8},{16,12},{20,16},{24,20},{28,24},{0,28},{5,1},{9... | collective-permute-start | bytes 49160 | tf_op jit(solution)/shard_map/ppermute | solution.py:41
  17.1 1.7 collective-permute-start.3
  19.4 3.0 collective-permute-done.2
  25.2 51.6 %reshape.179 = f32[12,2,16,2,128,2]{5,4,3,2,1,0:T(8,128)} reshape(f32[24,32,256]{2,1,0:T(8,128)S(1)} %pad_maximum_fusion) | data formatting | bytes 1572864 | tf_op jit(solution)/shard_map/reshape | solution.py:99
  76.8 17.8 %reduce_sum.98 = f32[12,16,128]{2,1,0:T(8,128)S(1)} reduce(f32[12,2,16,2,128,2]{5,4,3,2,1,0:T(8,128)} %reshape.179, f32[]{:T(128)} %constant.162.clone.1), dimensions={1,3,5}, to_apply=%region_1.2 | reduce | flops 172032 | bytes 884740 | tf_op jit(solution)/shard_map/reduce_sum | solution.py:102
  95.4 7.7 %mul.837 = f32[6,2,8,2,64,2]{5,4,3,2,1,0:T(8,128)} reshape(f32[12,16,128]{2,1,0:T(8,128)S(1)} %broadcast_multiply_fusion) | data formatting | bytes 196608 | tf_op jit(solution)/shard_map/mul | solution.py:102
  103.0 3.3 reduce_sum.100
  108.6 5.3 %all_gather.10 = f32[1,8,32]{2,0,1:T(1,128)S(1)} all-gather(f32[1,2,32]{2,0,1:T(1,128)S(1)} %bitcast.82), channel_id=1, replica_groups=mesh['tx'=8,'ty'=4] {'ty'}, dimensions={1}, use_global_device_ids=true | all-gather | bytes 1280 | tf_op jit(solution)/shard_map/all_gather | solution.py:177
  114.0 30.6 %all_gather.11 = f32[8,8,32]{2,1,0:T(8,128)S(1)} all-gather(f32[1,8,32]{2,1,0:T(8,128)S(1)} %bitcast.76), channel_id=1, replica_groups=mesh['tx'=8,'ty'=4] {'tx'}, dimensions={0}, use_global_device_ids=true | all-gather | bytes 9216 | tf_op jit(solution)/shard_map/all_gather | solution.py:181
  147.2 2.1 collective-permute-start.8
  150.3 2.9 cholesky.16
  156.1 1.5 fusion.178
  159.7 1.8 collective-permute-done.11
  161.7 4.8 %collective-permute-start.12 = (f32[1,16,256]{2,1,0:T(8,128)S(1)}, f32[1,16,256]{2,1,0:T(8,128)S(1)}, u32[]{:S(2)}, u32[]{:S(2)}) collective-permute-start(f32[1,16,256]{2,1,0:T(8,128)S(1)} %get-tuple-element.96), channel_id=1, source_target_pairs={{4,0},{8,4},{12,8},{16,12},{20,16},{24,20},{28,24},{0,28},{5,1},{9... | collective-permute-start | bytes 49160 | tf_op jit(solution)/shard_map/ppermute | solution.py:41
  168.0 5.0 %collective-permute-done.13 = f32[1,16,256]{2,1,0:T(8,128)S(1)} collective-permute-done((f32[1,16,256]{2,1,0:T(8,128)S(1)}, f32[1,16,256]{2,1,0:T(8,128)S(1)}, u32[]{:S(2)}, u32[]{:S(2)}) %collective-permute-start.13) | collective-permute-done | bytes 16416 | tf_op jit(solution)/shard_map/ppermute | solution.py:39
  174.4 1.8 collective-permute-done.15
  176.5 9.8 %reshape.178 = f32[4,2,8,2,128,2]{5,4,3,2,1,0:T(8,128)} reshape(f32[8,16,256]{2,1,0:T(8,128)S(1)} %fusion.92) | data formatting | bytes 262144 | tf_op jit(solution)/shard_map/reshape | solution.py:99
  186.3 4.0 %reduce_sum.97 = f32[4,8,128]{2,1,0:T(8,128)S(1)} reduce(f32[4,2,8,2,128,2]{5,4,3,2,1,0:T(8,128)} %reshape.178, f32[]{:T(128)} %constant.162.clone.1), dimensions={1,3,5}, to_apply=%region_0.1 | reduce | flops 28672 | bytes 147460 | tf_op jit(solution)/shard_map/reduce_sum | solution.py:102
  190.4 2.0 collective-permute-start.17
  192.5 1.5 collective-permute-done.16
  194.0 2.8 collective-permute-done.17
  198.1 1.8 collective-permute-done.19
  200.0 2.0 collective-permute-start.21
  202.1 1.5 collective-permute-done.20
  203.6 2.8 collective-permute-done.21
  207.7 1.9 collective-permute-done.23
  211.1 2.0 collective-permute-start.25
  213.2 1.5 collective-permute-done.24
  214.7 2.8 collective-permute-done.25
  218.8 1.8 collective-permute-done.27
  221.4 2.0 collective-permute-start.29
  225.0 2.8 collective-permute-done.29
  229.1 1.8 collective-permute-done.31
  231.9 5.1 %all-gather.1 = f32[4,2,32]{2,1,0:T(2,128)S(1)} all-gather(f32[1,2,32]{2,1,0:T(2,128)S(1)} %multiply_bitcast_fusion), channel_id=2, replica_groups=mesh['tx'=8,'ty'=4] {'ty'}, dimensions={0}, use_global_device_ids=true | all-gather | bytes 1280 | tf_op jit(solution)/shard_map/all_gather | solution.py:176
  237.6 4.7 %collective-permute-start.33 = (f32[1,8,32]{2,1,0:T(8,128)S(1)}, f32[1,8,32]{2,1,0:T(8,128)S(1)}, u32[]{:S(2)}, u32[]{:S(2)}) collective-permute-start(f32[1,8,32]{2,1,0:T(8,128)S(1)} %bitcast.74), channel_id=1, source_target_pairs={{0,28},{4,0},{8,4},{12,8},{16,12},{20,16},{24,20},{28,24},{1,29},{... | collective-permute-start | bytes 3080 | tf_op jit(solution)/shard_map/ppermute | solution.py:25
  243.6 5.0 %collective-permute-start.35 = (f32[1,8,32]{2,1,0:T(8,128)S(1)}, f32[1,8,32]{2,1,0:T(8,128)S(1)}, u32[]{:S(2)}, u32[]{:S(2)}) collective-permute-start(f32[1,8,32]{2,1,0:T(8,128)S(1)} %collective-permute-done.33), channel_id=1, source_target_pairs={{0,28},{4,0},{8,4},{12,8},{16,12},{20,16},{24,20},{28,24},{1,29},{... | collective-permute-start | bytes 3080 | tf_op jit(solution)/shard_map/ppermute | solution.py:25
  252.4 1.6 copy.839
  254.0 4.7 %collective-permute-start.37 = (f32[1,8,32]{2,1,0:T(8,128)S(1)}, f32[1,8,32]{2,1,0:T(8,128)S(1)}, u32[]{:S(2)}, u32[]{:S(2)}) collective-permute-start(f32[1,8,32]{2,1,0:T(8,128)S(1)} %collective-permute-done.35), channel_id=1, source_target_pairs={{0,28},{4,0},{8,4},{12,8},{16,12},{20,16},{24,20},{28,24},{1,29},{... | collective-permute-start | bytes 3080 | tf_op jit(solution)/shard_map/ppermute | solution.py:25
  260.2 3.2 custom-call.10
  274.4 4.3 %collective-permute-start.39 = (f32[1,4,64]{2,1,0:T(4,128)S(1)}, f32[1,4,64]{2,1,0:T(4,128)S(1)}, u32[]{:S(2)}, u32[]{:S(2)}) collective-permute-start(f32[1,4,64]{2,1,0:T(4,128)S(1)} %get-tuple-element.228), channel_id=1, source_target_pairs={{4,0},{8,4},{12,8},{16,12},{20,16},{24,20},{28,24},{0,28},{5,1},{9... | collective-permute-start | bytes 3080 | tf_op jit(solution)/shard_map/ppermute | solution.py:41
  280.0 5.0 %collective-permute-done.40 = f32[1,4,64]{2,1,0:T(4,128)S(1)} collective-permute-done((f32[1,4,64]{2,1,0:T(4,128)S(1)}, f32[1,4,64]{2,1,0:T(4,128)S(1)}, u32[]{:S(2)}, u32[]{:S(2)}) %collective-permute-start.40) | collective-permute-done | bytes 1056 | tf_op jit(solution)/shard_map/ppermute | solution.py:39
  286.3 1.8 collective-permute-done.42
  289.0 2.0 collective-permute-start.44
  291.1 1.5 collective-permute-done.43
  292.6 2.8 collective-permute-done.44
  296.8 1.8 collective-permute-done.46
  299.8 2.0 collective-permute-start.48
  301.8 1.5 collective-permute-done.47
  303.4 2.8 collective-permute-done.48
  307.4 1.8 collective-permute-done.50
  310.2 2.0 collective-permute-start.52
  312.3 1.5 collective-permute-done.51
  313.8 2.8 collective-permute-done.52
  317.9 1.8 collective-permute-done.54
  321.4 2.0 collective-permute-start.56
  323.5 1.6 collective-permute-done.55
  325.2 2.8 collective-permute-done.56
  329.4 1.8 collective-permute-done.58
  331.5 2.0 collective-permute-start.60
  333.6 1.6 collective-permute-done.59
  335.2 2.8 collective-permute-done.60
  339.4 1.8 collective-permute-done.62
  (371 shorter events, 68.8 us)
Async XLA Ops:
  1.0 15.9 %collective-permute-start = (f32[8,16,256]{2,1,0:T(8,128)S(1)}, f32[8,16,256]{2,1,0:T(8,128)S(1)}, u32[]{:S(2)}, u32[]{:S(2)}) collective-permute-start(f32[8,16,256]{2,1,0:T(8,128)S(1)} %select_select_fusion), channel_id=1, source_target_pairs={{0,4},{4,8},{8,12},{12,16},{16,20},{20,24},{24,28},{28,0},{1,5},{5... | collective-permute-start | bytes 393224 | tf_op jit(solution)/shard_map/ppermute | solution.py:39
  4.1 12.9 %collective-permute-start.1 = (f32[8,16,256]{2,1,0:T(8,128)S(1)}, f32[8,16,256]{2,1,0:T(8,128)S(1)}, u32[]{:S(2)}, u32[]{:S(2)}) collective-permute-start(f32[8,16,256]{2,1,0:T(8,128)S(1)} %select_select_fusion), channel_id=1, source_target_pairs={{4,0},{8,4},{12,8},{16,12},{20,16},{24,20},{28,24},{0,28},{5,1},{9... | collective-permute-start | bytes 393224 | tf_op jit(solution)/shard_map/ppermute | solution.py:41
  7.9 8.1 %collective-permute-start.5 = (f32[1,16,256]{2,1,0:T(8,128)S(1)}, f32[1,16,256]{2,1,0:T(8,128)S(1)}, u32[]{:S(2)}, u32[]{:S(2)}) collective-permute-start(f32[1,16,256]{2,1,0:T(8,128)S(1)} %get-tuple-element.108), channel_id=1, source_target_pairs={{0,4},{4,8},{8,12},{12,16},{16,20},{20,24},{24,28},{28,0},{1,5},{5... | collective-permute-start | bytes 49160 | tf_op jit(solution)/shard_map/ppermute | solution.py:39
  7.9 9.0 %collective-permute-start.4 = (f32[1,16,256]{2,1,0:T(8,128)S(1)}, f32[1,16,256]{2,1,0:T(8,128)S(1)}, u32[]{:S(2)}, u32[]{:S(2)}) collective-permute-start(f32[1,16,256]{2,1,0:T(8,128)S(1)} %get-tuple-element.107), channel_id=1, source_target_pairs={{4,0},{8,4},{12,8},{16,12},{20,16},{24,20},{28,24},{0,28},{5,1},{9... | collective-permute-start | bytes 49160 | tf_op jit(solution)/shard_map/ppermute | solution.py:41
  17.0 5.4 %collective-permute-start.2 = (f32[24,8,256]{2,1,0:T(8,128)S(1)}, f32[24,8,256]{2,1,0:T(8,128)S(1)}, u32[]{:S(2)}, u32[]{:S(2)}) collective-permute-start(f32[24,8,256]{2,1,0:T(8,128)S(1)} %get-tuple-element.35), channel_id=1, source_target_pairs={{0,1},{1,2},{2,3},{3,0},{4,5},{5,6},{6,7},{7,4},{8,9},{9,10},{10,1... | collective-permute-start | bytes 589832 | tf_op jit(solution)/shard_map/ppermute | solution.py:39
  17.1 6.4 %collective-permute-start.3 = (f32[24,8,256]{2,1,0:T(8,128)S(1)}, f32[24,8,256]{2,1,0:T(8,128)S(1)}, u32[]{:S(2)}, u32[]{:S(2)}) collective-permute-start(f32[24,8,256]{2,1,0:T(8,128)S(1)} %get-tuple-element.36), channel_id=1, source_target_pairs={{1,0},{2,1},{3,2},{0,3},{5,4},{6,5},{7,6},{4,7},{9,8},{10,9},{11,1... | collective-permute-start | bytes 589832 | tf_op jit(solution)/shard_map/ppermute | solution.py:41
  18.9 5.2 %collective-permute-start.6 = (f32[10,1,256]{2,1,0:T(1,128)S(1)}, f32[10,1,256]{2,1,0:T(1,128)S(1)}, u32[]{:S(2)}, u32[]{:S(2)}) collective-permute-start(f32[10,1,256]{2,1,0:T(1,128)S(1)} %get-tuple-element.53), channel_id=1, source_target_pairs={{1,0},{2,1},{3,2},{0,3},{5,4},{6,5},{7,6},{4,7},{9,8},{10,9},{11,1... | collective-permute-start | bytes 30728 | tf_op jit(solution)/shard_map/ppermute | solution.py:41
  18.9 5.2 %collective-permute-start.7 = (f32[10,1,256]{2,1,0:T(1,128)S(1)}, f32[10,1,256]{2,1,0:T(1,128)S(1)}, u32[]{:S(2)}, u32[]{:S(2)}) collective-permute-start(f32[10,1,256]{2,1,0:T(1,128)S(1)} %get-tuple-element.54), channel_id=1, source_target_pairs={{0,1},{1,2},{2,3},{3,0},{4,5},{5,6},{6,7},{7,4},{8,9},{9,10},{10,1... | collective-permute-start | bytes 30728 | tf_op jit(solution)/shard_map/ppermute | solution.py:39
  147.2 11.1 %collective-permute-start.8 = (f32[1,16,256]{2,1,0:T(8,128)}, f32[1,16,256]{2,1,0:T(8,128)S(1)}, u32[]{:S(2)}, u32[]{:S(2)}) collective-permute-start(f32[1,16,256]{2,1,0:T(8,128)} %get-tuple-element.102), channel_id=1, source_target_pairs={{4,0},{8,4},{12,8},{16,12},{20,16},{24,20},{28,24},{0,28},{5,1},{9... | collective-permute-start | bytes 49160 | tf_op jit(solution)/shard_map/ppermute | solution.py:41
  149.3 8.9 %collective-permute-start.9 = (f32[1,16,256]{2,1,0:T(8,128)}, f32[1,16,256]{2,1,0:T(8,128)S(1)}, u32[]{:S(2)}, u32[]{:S(2)}) collective-permute-start(f32[1,16,256]{2,1,0:T(8,128)} %get-tuple-element.101), channel_id=1, source_target_pairs={{0,4},{4,8},{8,12},{12,16},{16,20},{20,24},{24,28},{28,0},{1,5},{5... | collective-permute-start | bytes 49160 | tf_op jit(solution)/shard_map/ppermute | solution.py:39
  157.6 73.3 %copy-start.15 = (f32[4,6,64]{2,1,0:T(8,128)}, f32[4,6,64]{2,1,0:T(8,128)S(1)}, u32[]{:S(2)}) copy-start(f32[4,6,64]{2,1,0:T(8,128)S(1)} %get-tuple-element.136) | copy-start | bytes 18436
  158.3 1.4 collective-permute-start.10
  158.3 3.1 collective-permute-start.11
  161.7 6.2 %collective-permute-start.12 = (f32[1,16,256]{2,1,0:T(8,128)S(1)}, f32[1,16,256]{2,1,0:T(8,128)S(1)}, u32[]{:S(2)}, u32[]{:S(2)}) collective-permute-start(f32[1,16,256]{2,1,0:T(8,128)S(1)} %get-tuple-element.96), channel_id=1, source_target_pairs={{4,0},{8,4},{12,8},{16,12},{20,16},{24,20},{28,24},{0,28},{5,1},{9... | collective-permute-start | bytes 49160 | tf_op jit(solution)/shard_map/ppermute | solution.py:41
  166.5 6.4 %collective-permute-start.13 = (f32[1,16,256]{2,1,0:T(8,128)S(1)}, f32[1,16,256]{2,1,0:T(8,128)S(1)}, u32[]{:S(2)}, u32[]{:S(2)}) collective-permute-start(f32[1,16,256]{2,1,0:T(8,128)S(1)} %get-tuple-element.95), channel_id=1, source_target_pairs={{0,4},{4,8},{8,12},{12,16},{16,20},{20,24},{24,28},{28,0},{1,5},{5... | collective-permute-start | bytes 49160 | tf_op jit(solution)/shard_map/ppermute | solution.py:39
  173.0 1.4 collective-permute-start.14
  173.0 3.1 collective-permute-start.15
  190.4 3.7 %collective-permute-start.16 = (f32[1,8,128]{2,1,0:T(8,128)S(1)}, f32[1,8,128]{2,1,0:T(8,128)S(1)}, u32[]{:S(2)}, u32[]{:S(2)}) collective-permute-start(f32[1,8,128]{2,1,0:T(8,128)S(1)} %get-tuple-element.178), channel_id=1, source_target_pairs={{4,0},{8,4},{12,8},{16,12},{20,16},{24,20},{28,24},{0,28},{5,1},{9... | collective-permute-start | bytes 12296 | tf_op jit(solution)/shard_map/ppermute | solution.py:41
  190.4 6.4 %collective-permute-start.17 = (f32[1,8,128]{2,1,0:T(8,128)S(1)}, f32[1,8,128]{2,1,0:T(8,128)S(1)}, u32[]{:S(2)}, u32[]{:S(2)}) collective-permute-start(f32[1,8,128]{2,1,0:T(8,128)S(1)} %get-tuple-element.177), channel_id=1, source_target_pairs={{0,4},{4,8},{8,12},{12,16},{16,20},{20,24},{24,28},{28,0},{1,5},{5... | collective-permute-start | bytes 12296 | tf_op jit(solution)/shard_map/ppermute | solution.py:39
  196.8 1.3 collective-permute-start.18
  196.8 3.1 collective-permute-start.19
  200.0 3.7 %collective-permute-start.20 = (f32[1,8,128]{2,1,0:T(8,128)S(1)}, f32[1,8,128]{2,1,0:T(8,128)S(1)}, u32[]{:S(2)}, u32[]{:S(2)}) collective-permute-start(f32[1,8,128]{2,1,0:T(8,128)S(1)} %get-tuple-element.172), channel_id=1, source_target_pairs={{4,0},{8,4},{12,8},{16,12},{20,16},{24,20},{28,24},{0,28},{5,1},{9... | collective-permute-start | bytes 12296 | tf_op jit(solution)/shard_map/ppermute | solution.py:41
  200.0 6.4 %collective-permute-start.21 = (f32[1,8,128]{2,1,0:T(8,128)S(1)}, f32[1,8,128]{2,1,0:T(8,128)S(1)}, u32[]{:S(2)}, u32[]{:S(2)}) collective-permute-start(f32[1,8,128]{2,1,0:T(8,128)S(1)} %get-tuple-element.171), channel_id=1, source_target_pairs={{0,4},{4,8},{8,12},{12,16},{16,20},{20,24},{24,28},{28,0},{1,5},{5... | collective-permute-start | bytes 12296 | tf_op jit(solution)/shard_map/ppermute | solution.py:39
  206.4 1.3 collective-permute-start.22
  206.4 3.3 collective-permute-start.23
  211.0 3.6 %collective-permute-start.24 = (f32[1,4,64]{2,1,0:T(4,128)S(1)}, f32[1,4,64]{2,1,0:T(4,128)S(1)}, u32[]{:S(2)}, u32[]{:S(2)}) collective-permute-start(f32[1,4,64]{2,1,0:T(4,128)S(1)} %get-tuple-element.242), channel_id=1, source_target_pairs={{4,0},{8,4},{12,8},{16,12},{20,16},{24,20},{28,24},{0,28},{5,1},{9... | collective-permute-start | bytes 3080 | tf_op jit(solution)/shard_map/ppermute | solution.py:41
  211.1 6.3 %collective-permute-start.25 = (f32[1,4,64]{2,1,0:T(4,128)S(1)}, f32[1,4,64]{2,1,0:T(4,128)S(1)}, u32[]{:S(2)}, u32[]{:S(2)}) collective-permute-start(f32[1,4,64]{2,1,0:T(4,128)S(1)} %get-tuple-element.241), channel_id=1, source_target_pairs={{0,4},{4,8},{8,12},{12,16},{16,20},{20,24},{24,28},{28,0},{1,5},{5... | collective-permute-start | bytes 3080 | tf_op jit(solution)/shard_map/ppermute | solution.py:39
  217.4 1.4 collective-permute-start.26
  217.5 3.1 collective-permute-start.27
  221.4 3.6 %collective-permute-start.28 = (f32[1,4,64]{2,1,0:T(4,128)S(1)}, f32[1,4,64]{2,1,0:T(4,128)S(1)}, u32[]{:S(2)}, u32[]{:S(2)}) collective-permute-start(f32[1,4,64]{2,1,0:T(4,128)S(1)} %get-tuple-element.232), channel_id=1, source_target_pairs={{4,0},{8,4},{12,8},{16,12},{20,16},{24,20},{28,24},{0,28},{5,1},{9... | collective-permute-start | bytes 3080 | tf_op jit(solution)/shard_map/ppermute | solution.py:41
  221.4 6.3 %collective-permute-start.29 = (f32[1,4,64]{2,1,0:T(4,128)S(1)}, f32[1,4,64]{2,1,0:T(4,128)S(1)}, u32[]{:S(2)}, u32[]{:S(2)}) collective-permute-start(f32[1,4,64]{2,1,0:T(4,128)S(1)} %get-tuple-element.231), channel_id=1, source_target_pairs={{0,4},{4,8},{8,12},{12,16},{16,20},{20,24},{24,28},{28,0},{1,5},{5... | collective-permute-start | bytes 3080 | tf_op jit(solution)/shard_map/ppermute | solution.py:39
  227.8 1.4 collective-permute-start.30
  227.8 3.1 collective-permute-start.31
  237.0 6.3 %collective-permute-start.32 = (f32[1,8,32]{2,1,0:T(8,128)S(1)}, f32[1,8,32]{2,1,0:T(8,128)S(1)}, u32[]{:S(2)}, u32[]{:S(2)}) collective-permute-start(f32[1,8,32]{2,1,0:T(8,128)S(1)} %bitcast.73), channel_id=1, source_target_pairs={{0,4},{4,8},{8,12},{12,16},{16,20},{20,24},{24,28},{28,0},{1,5},{5... | collective-permute-start | bytes 3080 | tf_op jit(solution)/shard_map/ppermute | solution.py:20
  237.6 6.0 %collective-permute-start.33 = (f32[1,8,32]{2,1,0:T(8,128)S(1)}, f32[1,8,32]{2,1,0:T(8,128)S(1)}, u32[]{:S(2)}, u32[]{:S(2)}) collective-permute-start(f32[1,8,32]{2,1,0:T(8,128)S(1)} %bitcast.74), channel_id=1, source_target_pairs={{0,28},{4,0},{8,4},{12,8},{16,12},{20,16},{24,20},{28,24},{1,29},{... | collective-permute-start | bytes 3080 | tf_op jit(solution)/shard_map/ppermute | solution.py:25
  243.3 6.3 %collective-permute-start.34 = (f32[1,8,32]{2,1,0:T(8,128)S(1)}, f32[1,8,32]{2,1,0:T(8,128)S(1)}, u32[]{:S(2)}, u32[]{:S(2)}) collective-permute-start(f32[1,8,32]{2,1,0:T(8,128)S(1)} %collective-permute-done.32), channel_id=1, source_target_pairs={{0,4},{4,8},{8,12},{12,16},{16,20},{20,24},{24,28},{28,0},{1,5},{5... | collective-permute-start | bytes 3080 | tf_op jit(solution)/shard_map/ppermute | solution.py:20
  243.6 10.3 %collective-permute-start.35 = (f32[1,8,32]{2,1,0:T(8,128)S(1)}, f32[1,8,32]{2,1,0:T(8,128)S(1)}, u32[]{:S(2)}, u32[]{:S(2)}) collective-permute-start(f32[1,8,32]{2,1,0:T(8,128)S(1)} %collective-permute-done.33), channel_id=1, source_target_pairs={{0,28},{4,0},{8,4},{12,8},{16,12},{20,16},{24,20},{28,24},{1,29},{... | collective-permute-start | bytes 3080 | tf_op jit(solution)/shard_map/ppermute | solution.py:25
  249.6 9.1 %collective-permute-start.36 = (f32[1,8,32]{2,1,0:T(8,128)S(1)}, f32[1,8,32]{2,1,0:T(8,128)S(1)}, u32[]{:S(2)}, u32[]{:S(2)}) collective-permute-start(f32[1,8,32]{2,1,0:T(8,128)S(1)} %collective-permute-done.34), channel_id=1, source_target_pairs={{0,4},{4,8},{8,12},{12,16},{16,20},{20,24},{24,28},{28,0},{1,5},{5... | collective-permute-start | bytes 3080 | tf_op jit(solution)/shard_map/ppermute | solution.py:20
  254.0 10.4 %collective-permute-start.37 = (f32[1,8,32]{2,1,0:T(8,128)S(1)}, f32[1,8,32]{2,1,0:T(8,128)S(1)}, u32[]{:S(2)}, u32[]{:S(2)}) collective-permute-start(f32[1,8,32]{2,1,0:T(8,128)S(1)} %collective-permute-done.35), channel_id=1, source_target_pairs={{0,28},{4,0},{8,4},{12,8},{16,12},{20,16},{24,20},{28,24},{1,29},{... | collective-permute-start | bytes 3080 | tf_op jit(solution)/shard_map/ppermute | solution.py:25
  258.7 6.3 %collective-permute-start.38 = (f32[1,8,32]{2,1,0:T(8,128)S(1)}, f32[1,8,32]{2,1,0:T(8,128)S(1)}, u32[]{:S(2)}, u32[]{:S(2)}) collective-permute-start(f32[1,8,32]{2,1,0:T(8,128)S(1)} %collective-permute-done.36), channel_id=1, source_target_pairs={{0,4},{4,8},{8,12},{12,16},{16,20},{20,24},{24,28},{28,0},{1,5},{5... | collective-permute-start | bytes 3080 | tf_op jit(solution)/shard_map/ppermute | solution.py:20
  274.4 5.6 %collective-permute-start.39 = (f32[1,4,64]{2,1,0:T(4,128)S(1)}, f32[1,4,64]{2,1,0:T(4,128)S(1)}, u32[]{:S(2)}, u32[]{:S(2)}) collective-permute-start(f32[1,4,64]{2,1,0:T(4,128)S(1)} %get-tuple-element.228), channel_id=1, source_target_pairs={{4,0},{8,4},{12,8},{16,12},{20,16},{24,20},{28,24},{0,28},{5,1},{9... | collective-permute-start | bytes 3080 | tf_op jit(solution)/shard_map/ppermute | solution.py:41
  278.7 6.3 %collective-permute-start.40 = (f32[1,4,64]{2,1,0:T(4,128)S(1)}, f32[1,4,64]{2,1,0:T(4,128)S(1)}, u32[]{:S(2)}, u32[]{:S(2)}) collective-permute-start(f32[1,4,64]{2,1,0:T(4,128)S(1)} %get-tuple-element.227), channel_id=1, source_target_pairs={{0,4},{4,8},{8,12},{12,16},{16,20},{20,24},{24,28},{28,0},{1,5},{5... | collective-permute-start | bytes 3080 | tf_op jit(solution)/shard_map/ppermute | solution.py:39
  285.0 1.4 collective-permute-start.41
  285.0 3.1 collective-permute-start.42
  289.0 3.6 %collective-permute-start.43 = (f32[1,4,64]{2,1,0:T(4,128)S(1)}, f32[1,4,64]{2,1,0:T(4,128)S(1)}, u32[]{:S(2)}, u32[]{:S(2)}) collective-permute-start(f32[1,4,64]{2,1,0:T(4,128)S(1)} %get-tuple-element.222), channel_id=1, source_target_pairs={{4,0},{8,4},{12,8},{16,12},{20,16},{24,20},{28,24},{0,28},{5,1},{9... | collective-permute-start | bytes 3080 | tf_op jit(solution)/shard_map/ppermute | solution.py:41
  289.0 6.3 %collective-permute-start.44 = (f32[1,4,64]{2,1,0:T(4,128)S(1)}, f32[1,4,64]{2,1,0:T(4,128)S(1)}, u32[]{:S(2)}, u32[]{:S(2)}) collective-permute-start(f32[1,4,64]{2,1,0:T(4,128)S(1)} %get-tuple-element.221), channel_id=1, source_target_pairs={{0,4},{4,8},{8,12},{12,16},{16,20},{20,24},{24,28},{28,0},{1,5},{5... | collective-permute-start | bytes 3080 | tf_op jit(solution)/shard_map/ppermute | solution.py:39
  295.4 1.4 collective-permute-start.45
  295.5 3.1 collective-permute-start.46
  299.7 3.7 %collective-permute-start.47 = (f32[1,8,128]{2,1,0:T(8,128)S(1)}, f32[1,8,128]{2,1,0:T(8,128)S(1)}, u32[]{:S(2)}, u32[]{:S(2)}) collective-permute-start(f32[1,8,128]{2,1,0:T(8,128)S(1)} %get-tuple-element.160), channel_id=1, source_target_pairs={{4,0},{8,4},{12,8},{16,12},{20,16},{24,20},{28,24},{0,28},{5,1},{9... | collective-permute-start | bytes 12296 | tf_op jit(solution)/shard_map/ppermute | solution.py:41
  299.8 6.4 %collective-permute-start.48 = (f32[1,8,128]{2,1,0:T(8,128)S(1)}, f32[1,8,128]{2,1,0:T(8,128)S(1)}, u32[]{:S(2)}, u32[]{:S(2)}) collective-permute-start(f32[1,8,128]{2,1,0:T(8,128)S(1)} %get-tuple-element.159), channel_id=1, source_target_pairs={{0,4},{4,8},{8,12},{12,16},{16,20},{20,24},{24,28},{28,0},{1,5},{5... | collective-permute-start | bytes 12296 | tf_op jit(solution)/shard_map/ppermute | solution.py:39
  306.1 1.3 collective-permute-start.49
  306.1 3.1 collective-permute-start.50
  310.1 3.7 %collective-permute-start.51 = (f32[1,8,128]{2,1,0:T(8,128)S(1)}, f32[1,8,128]{2,1,0:T(8,128)S(1)}, u32[]{:S(2)}, u32[]{:S(2)}) collective-permute-start(f32[1,8,128]{2,1,0:T(8,128)S(1)} %get-tuple-element.154), channel_id=1, source_target_pairs={{4,0},{8,4},{12,8},{16,12},{20,16},{24,20},{28,24},{0,28},{5,1},{9... | collective-permute-start | bytes 12296 | tf_op jit(solution)/shard_map/ppermute | solution.py:41
  310.2 6.4 %collective-permute-start.52 = (f32[1,8,128]{2,1,0:T(8,128)S(1)}, f32[1,8,128]{2,1,0:T(8,128)S(1)}, u32[]{:S(2)}, u32[]{:S(2)}) collective-permute-start(f32[1,8,128]{2,1,0:T(8,128)S(1)} %get-tuple-element.153), channel_id=1, source_target_pairs={{0,4},{4,8},{8,12},{12,16},{16,20},{20,24},{24,28},{28,0},{1,5},{5... | collective-permute-start | bytes 12296 | tf_op jit(solution)/shard_map/ppermute | solution.py:39
  316.6 1.3 collective-permute-start.53
  316.6 3.1 collective-permute-start.54
  321.4 3.8 %collective-permute-start.55 = (f32[1,16,256]{2,1,0:T(8,128)S(1)}, f32[1,16,256]{2,1,0:T(8,128)S(1)}, u32[]{:S(2)}, u32[]{:S(2)}) collective-permute-start(f32[1,16,256]{2,1,0:T(8,128)S(1)} %get-tuple-element.66), channel_id=1, source_target_pairs={{4,0},{8,4},{12,8},{16,12},{20,16},{24,20},{28,24},{0,28},{5,1},{9... | collective-permute-start | bytes 49160 | tf_op jit(solution)/shard_map/ppermute | solution.py:41
  321.4 6.5 %collective-permute-start.56 = (f32[1,16,256]{2,1,0:T(8,128)S(1)}, f32[1,16,256]{2,1,0:T(8,128)S(1)}, u32[]{:S(2)}, u32[]{:S(2)}) collective-permute-start(f32[1,16,256]{2,1,0:T(8,128)S(1)} %get-tuple-element.65), channel_id=1, source_target_pairs={{0,4},{4,8},{8,12},{12,16},{16,20},{20,24},{24,28},{28,0},{1,5},{5... | collective-permute-start | bytes 49160 | tf_op jit(solution)/shard_map/ppermute | solution.py:39
  327.9 1.4 collective-permute-start.57
  328.0 3.1 collective-permute-start.58
  331.4 3.8 %collective-permute-start.59 = (f32[1,16,256]{2,1,0:T(8,128)S(1)}, f32[1,16,256]{2,1,0:T(8,128)S(1)}, u32[]{:S(2)}, u32[]{:S(2)}) collective-permute-start(f32[1,16,256]{2,1,0:T(8,128)S(1)} %get-tuple-element.60), channel_id=1, source_target_pairs={{4,0},{8,4},{12,8},{16,12},{20,16},{24,20},{28,24},{0,28},{5,1},{9... | collective-permute-start | bytes 49160 | tf_op jit(solution)/shard_map/ppermute | solution.py:41
  331.5 6.5 %collective-permute-start.60 = (f32[1,16,256]{2,1,0:T(8,128)S(1)}, f32[1,16,256]{2,1,0:T(8,128)S(1)}, u32[]{:S(2)}, u32[]{:S(2)}) collective-permute-start(f32[1,16,256]{2,1,0:T(8,128)S(1)} %get-tuple-element.59), channel_id=1, source_target_pairs={{0,4},{4,8},{8,12},{12,16},{16,20},{20,24},{24,28},{28,0},{1,5},{5... | collective-permute-start | bytes 49160 | tf_op jit(solution)/shard_map/ppermute | solution.py:39
  338.0 1.4 collective-permute-start.61
  338.0 3.1 collective-permute-start.62
  (29 other events, 1368.1 us)
